TPU v7x, 128 devices: a whole 4x4x4 slice. The times are simulated.
128 devices in a mesh: patch: 2 (over core), cells: 64 (over y, x, z).
Axes of the slice: x: 4, y: 4, z: 4, core: 2. Of those that a mesh axis runs over, the one named last changes fastest.
Arguments:
- features: bfloat16 [128, 1024, 512], P('cells', 'patch'), may hold values from -6 to 6
- hilbert_rank: int32 [128, 32], P('cells', 'patch'), may hold values from 0 to 4095, as said below
- valid_count: int32 [128, 32], P('cells', 'patch'), may hold values from 1 to 32
- norm_gains: float32 [3, 512], replicated
- w_qkv: bfloat16 [512, 1536], replicated
- w_out: bfloat16 [512, 512], replicated, may hold values from -0.25 to 0.25
- w_up: bfloat16 [2, 512, 2048], replicated, may hold values from -0.25 to 0.25
- w_down: bfloat16 [2, 2048, 512], replicated, may hold values from -0.125 to 0.125
Outputs:
- final: bfloat16 [128, 1024, 512], P('cells', 'patch')
Inputs may be any that keep to these rules, and one draw needn't show every extreme that they name: `hilbert_rank`: a permutation of all cells; a cell keeps its half of a patch (its index within the patch divided by 16 stays the same); the 32 cells of one device go to exactly 32 owners along cells (the device itself may be one), 1 cells to each.
All inputs are finite; a program needn't handle non-finite values.
Results may differ from a plain program's by a relative error of at most 0.013.
The roundings to bfloat16 on the way count: a program that leaves them out, or rounds other values in their place, can miss the bound.
Values may be sent and summed in bfloat16 or wider, within the bound.
A program may use at most 128 MiB of HBM per device.

v0:
```python
import functools
import itertools
import random

import jax
import jax.numpy as jnp
from jax import lax
from jax.experimental import pallas as pl
from jax.experimental.pallas import tpu as pltpu
from jax.sharding import PartitionSpec as P

MESH = pl.DeviceIdType.MESH
EPSILON = 1e-05
C = 512
FF = 2048
CELL = 32
SIDE = 4
SLOTS = SIDE**3
CELLS_DEV = 32
HALF_CELLS = 16
HALF_ROWS = 512
PATCH_ROWS = 1024
GROUPS = 4
GROUP_LANES = 128
GROUP_HEADS = 8
DEPTH = 16
TM = 128
TQ = 64
TK = 128
VMEM_LIMIT = 60 * 1024 * 1024

OFFSETS = [o for o in itertools.product(range(SIDE), repeat=3) if o != (0, 0, 0)]
random.Random(0).shuffle(OFFSETS)


def slot_number(offset):
    return (offset[0] * SIDE + offset[1]) * SIDE + offset[2]


def coordinates():
    me = lax.axis_index("cells")
    return me // (SIDE * SIDE), (me // SIDE) % SIDE, me % SIDE


def peer(offset, sign):
    y, x, z = coordinates()
    ys = (y + sign * offset[0] + SIDE) % SIDE
    xs = (x + sign * offset[1] + SIDE) % SIDE
    zs = (z + sign * offset[2] + SIDE) % SIDE
    return (ys * SIDE + xs) * SIDE + zs


def norm_rows(values, gains):
    center = values - jnp.mean(values, axis=-1, keepdims=True)
    spread = jnp.mean(center * center, axis=-1, keepdims=True)
    return (center * lax.rsqrt(spread + EPSILON) * gains).astype(jnp.bfloat16)


def mlp_rows(rows, gain_row, w_up, w_down):
    normed = norm_rows(rows, gain_row)
    raised = jnp.dot(normed, w_up, preferred_element_type=jnp.float32)
    hidden = jax.nn.gelu(raised, approximate=True).astype(jnp.bfloat16)
    return rows + jnp.dot(hidden, w_down, preferred_element_type=jnp.float32)


def put_rows(ref, start, rows):
    base = pl.multiple_of(start // 8 * 8, 8)
    shift = start - base
    padded = jnp.concatenate([rows, jnp.zeros((8, C), jnp.float32)], axis=0)
    moved = pltpu.roll(padded, shift, 0)
    position = lax.broadcasted_iota(jnp.int32, (8, C), 0)
    ref[pl.ds(base, 8), :] = jnp.where(position < shift, ref[pl.ds(base, 8), :], moved[:8])
    ref[pl.ds(pl.multiple_of(base + 8, 8), CELL), :] = moved[8:]


def take_rows(ref, start):
    base = pl.multiple_of(start // 8 * 8, 8)
    window = ref[pl.ds(base, CELL + 8), :]
    ahead = start - base
    return pltpu.roll(window, jnp.where(ahead == 0, 0, CELL + 8 - ahead), 0)[:CELL]


def first_kernel(
    rank_ref, count_ref, features, gains, up_hbm, down_hbm,
    send, labels, slots, packed, w_up, w_down, offsets, slot_labels, sems,
):
    copies = [
        pltpu.make_async_copy(up_hbm.at[0], w_up, sems.at[0]),
        pltpu.make_async_copy(down_hbm.at[0], w_down, sems.at[1]),
    ]
    for copy in copies:
        copy.start()
    y, x, z = coordinates()

    def clear(slot, carry):
        slot_labels[slot] = 0
        return carry

    lax.fori_loop(0, SLOTS, clear, 0)

    def pack(cell, start):
        rank = rank_ref[cell // HALF_CELLS, cell % HALF_CELLS]
        count = count_ref[cell // HALF_CELLS, cell % HALF_CELLS]
        owner = rank // (2 * CELLS_DEV)
        patch = (rank // CELLS_DEV) % 2
        oy = (owner // (SIDE * SIDE) - y + SIDE) % SIDE
        ox = ((owner // SIDE) % SIDE - x + SIDE) % SIDE
        oz = (owner % SIDE - z + SIDE) % SIDE
        slot = (oy * SIDE + ox) * SIDE + oz
        slots[cell] = slot
        slot_labels[slot] = count + 64 * patch
        offsets[cell] = start
        cell_row = pl.multiple_of(cell * CELL, CELL)
        put_rows(packed, start, features[pl.ds(cell_row, CELL), :].astype(jnp.float32))
        return start + count

    total = lax.fori_loop(0, CELLS_DEV, pack, 0)

    def label(slot, carry):
        labels[slot] = jnp.full((1, 128), slot_labels[slot], jnp.int32)
        return carry

    lax.fori_loop(0, SLOTS, label, 0)
    for copy in copies:
        copy.wait()

    def tile(step, carry):
        rows = pl.ds(pl.multiple_of(step * TM, TM), TM)
        packed[rows, :] = mlp_rows(packed[rows, :], gains[0:1, :], w_up[...], w_down[...])
        return carry

    lax.fori_loop(0, (total + TM - 1) // TM, tile, 0)

    def unpack(cell, carry):
        send[slots[cell]] = take_rows(packed, offsets[cell]).astype(jnp.bfloat16)
        return carry

    lax.fori_loop(0, CELLS_DEV, unpack, 0)


def meet():
    core = lax.axis_index("patch")
    barrier = pltpu.get_barrier_semaphore()
    for offset in OFFSETS:
        pl.semaphore_signal(barrier, inc=1, device_id=(core, peer(offset, 1)), device_id_type=MESH)
    pl.semaphore_signal(
        barrier, inc=1, device_id=(1 - core, lax.axis_index("cells")), device_id_type=MESH
    )
    pl.semaphore_wait(barrier, SLOTS)


def forward_kernel(
    send, labels, own, other, own_labels, other_labels,
    arrived, arrived_labels, send_sem, recv_sem, label_send, label_recv,
    keep_sem, pass_sem, got_sem, tail_sem,
):
    core = lax.axis_index("patch")
    here = lax.axis_index("cells")
    sibling = (1 - core, here)
    meet()
    local = pltpu.make_async_copy(send.at[0], arrived.at[0], recv_sem.at[0])
    local_labels = pltpu.make_async_copy(labels.at[0], arrived_labels.at[0], label_recv.at[0])
    local.start()
    local_labels.start()
    copies = [local]
    label_copies = [local_labels]
    for offset in OFFSETS:
        slot = slot_number(offset)
        to = (core, peer(offset, 1))
        label_copy = pltpu.make_async_remote_copy(
            labels.at[slot], arrived_labels.at[slot], label_send.at[slot], label_recv.at[slot],
            device_id=to, device_id_type=MESH,
        )
        copy = pltpu.make_async_remote_copy(
            send.at[slot], arrived.at[slot], send_sem.at[slot], recv_sem.at[slot],
            device_id=to, device_id_type=MESH,
        )
        label_copy.start()
        copy.start()
        label_copies.append(label_copy)
        copies.append(copy)
    keeps = []
    passes = []
    for index, copy in enumerate(copies):
        slot = 0 if index == 0 else slot_number(OFFSETS[index - 1])
        if index == 0:
            copy.wait()
        else:
            copy.wait_recv()
        keep = pltpu.make_async_copy(arrived.at[slot], own.at[slot], keep_sem.at[slot])
        onward = pltpu.make_async_remote_copy(
            arrived.at[slot], other.at[slot], pass_sem.at[slot], got_sem.at[slot],
            device_id=sibling, device_id_type=MESH,
        )
        keep.start()
        onward.start()
        keeps.append(keep)
        passes.append(onward)
    for index, copy in enumerate(label_copies):
        if index == 0:
            copy.wait()
        else:
            copy.wait_recv()
    keep_labels = pltpu.make_async_copy(arrived_labels, own_labels, tail_sem.at[0])
    pass_labels = pltpu.make_async_remote_copy(
        arrived_labels, other_labels, tail_sem.at[1], tail_sem.at[2],
        device_id=sibling, device_id_type=MESH,
    )
    keep_labels.start()
    pass_labels.start()
    for copy in copies[1:]:
        copy.wait_send()
    for copy in label_copies[1:]:
        copy.wait_send()
    for keep in keeps:
        keep.wait()
    for onward in passes:
        onward.wait()
    keep_labels.wait()
    pass_labels.wait()


def layer_kernel(
    own_labels, other_labels, own, other, gains, qkv_hbm, out_hbm, up_hbm, down_hbm,
    send, packed, queries, keys, values, mixed, w_qkv, w_out, w_up, w_down, offsets, sems,
):
    copies = [
        pltpu.make_async_copy(qkv_hbm, w_qkv, sems.at[0]),
        pltpu.make_async_copy(out_hbm, w_out, sems.at[1]),
        pltpu.make_async_copy(up_hbm.at[1], w_up, sems.at[2]),
        pltpu.make_async_copy(down_hbm.at[1], w_down, sems.at[3]),
    ]
    for copy in copies:
        copy.start()

    def pack_own(slot, starts):
        label = own_labels[slot, 0]
        patch = label // 64
        count = label % 64
        start = jnp.where(patch == 0, starts[0], starts[1])

        @pl.when(count > 0)
        def _():
            offsets[slot] = start
            put_rows(packed.at[patch], start, own[slot].astype(jnp.float32))

        first = jnp.where(patch == 0, count, 0)
        return starts[0] + first, starts[1] + count - first

    query_rows = lax.fori_loop(0, SLOTS, pack_own, (jnp.int32(0), jnp.int32(0)))

    def pack_other(slot, starts):
        label = other_labels[slot, 0]
        patch = label // 64
        count = label % 64
        start = jnp.where(patch == 0, starts[0], starts[1])

        @pl.when(count > 0)
        def _():
            put_rows(packed.at[patch], start, other[slot].astype(jnp.float32))

        first = jnp.where(patch == 0, count, 0)
        return starts[0] + first, starts[1] + count - first

    key_rows = lax.fori_loop(0, SLOTS, pack_other, query_rows)
    for copy in copies:
        copy.wait()
    lane = lax.broadcasted_iota(jnp.int32, (1, GROUP_LANES), 1) // DEPTH
    head_masks = [(lane == head).astype(jnp.float32) for head in range(GROUP_HEADS)]

    def project(patch, key_count, step, carry):
        base = pl.multiple_of(step * TM, TM)
        rows = pl.ds(base, TM)
        normed = norm_rows(packed[patch, rows, :], gains[1:2, :])
        projected = jnp.dot(normed, w_qkv[...], preferred_element_type=jnp.float32)
        projected = projected.astype(jnp.bfloat16)
        seen = lax.broadcasted_iota(jnp.int32, (TM, GROUP_LANES), 0) + base < key_count
        for group in range(GROUPS):
            low = group * GROUP_LANES
            queries[group, rows, :] = projected[:, low : low + GROUP_LANES] * 0.25
            keys[group, rows, :] = projected[:, C + low : C + low + GROUP_LANES]
            value = projected[:, 2 * C + low : 2 * C + low + GROUP_LANES].astype(jnp.float32)
            values[group, rows, :GROUP_LANES] = jnp.where(seen, value, 0.0).astype(jnp.bfloat16)
            values[group, rows, GROUP_LANES:] = jnp.where(seen, 1.0, 0.0).astype(jnp.bfloat16)
        return carry

    def attend(key_span, step, carry):
        group = step % GROUPS
        rows = pl.ds(pl.multiple_of((step // GROUPS) * TQ, TQ), TQ)
        query = queries[group, rows, :].astype(jnp.float32)
        stacked = jnp.concatenate([query * mask for mask in head_masks], axis=0)
        scores = lax.dot_general(
            stacked.astype(jnp.bfloat16), keys[group, :key_span, :],
            (((1,), (1,)), ((), ())), preferred_element_type=jnp.float32,
        )
        highest = jnp.max(scores, axis=1, keepdims=True)
        weights = jnp.exp(scores - highest).astype(jnp.bfloat16)
        mixture = jnp.dot(weights, values[group, :key_span, :], preferred_element_type=jnp.float32)
        top = jnp.zeros((TQ, GROUP_LANES), jnp.float32)
        total = jnp.zeros((TQ, GROUP_LANES), jnp.float32)
        for head in range(GROUP_HEADS):
            part = mixture[head * TQ : (head + 1) * TQ, :]
            chosen = lane == head
            top = jnp.where(chosen, part[:, :GROUP_LANES], top)
            total = jnp.where(chosen, part[:, GROUP_LANES:], total)
        mixed[group, rows, :] = (top / total).astype(jnp.bfloat16)
        return carry

    def finish(patch, step, carry):
        rows = pl.ds(pl.multiple_of(step * TM, TM), TM)
        middle = packed[patch, rows, :]
        for group in range(GROUPS):
            low = group * GROUP_LANES
            middle = middle + jnp.dot(
                mixed[group, rows, :], w_out[low : low + GROUP_LANES, :],
                preferred_element_type=jnp.float32,
            )
        middle = middle.astype(jnp.bfloat16).astype(jnp.float32)
        packed[patch, rows, :] = mlp_rows(middle, gains[2:3, :], w_up[...], w_down[...])
        return carry

    def one_patch(patch, carry):
        query_count = jnp.where(patch == 0, query_rows[0], query_rows[1])
        key_count = jnp.where(patch == 0, key_rows[0], key_rows[1])
        base = pl.multiple_of(key_count // 8 * 8, 8)
        spare = jnp.broadcast_to(packed[patch, 0:1, :], (8, C))
        edge = packed[patch, pl.ds(base, 8), :]
        position = lax.broadcasted_iota(jnp.int32, (8, C), 0)
        packed[patch, pl.ds(base, 8), :] = jnp.where(position < key_count - base, edge, spare)
        packed[patch, pl.ds(pl.multiple_of(base + 8, 8), TK), :] = jnp.broadcast_to(spare[:1], (TK, C))
        key_tiles = (key_count + TK - 1) // TK
        lax.fori_loop(0, key_tiles, functools.partial(project, patch, key_count), 0)
        steps = (query_count + TQ - 1) // TQ * GROUPS
        for tiles in range(1, PATCH_ROWS // TK + 1):

            @pl.when(key_tiles == tiles)
            def _():
                lax.fori_loop(0, steps, functools.partial(attend, tiles * TK), 0)

        lax.fori_loop(0, (query_count + TM - 1) // TM, functools.partial(finish, patch), 0)
        return carry

    lax.fori_loop(0, 2, one_patch, 0)

    def unpack(slot, carry):
        label = own_labels[slot, 0]

        @pl.when(label > 0)
        def _():
            rows = take_rows(packed.at[label // 64], offsets[slot])
            send[slot] = rows.astype(jnp.bfloat16)

        return carry

    lax.fori_loop(0, SLOTS, unpack, 0)


def return_kernel(slots, counts, send, out, arrived, send_sem, recv_sem):
    core = lax.axis_index("patch")
    meet()
    local = pltpu.make_async_copy(send.at[0], arrived.at[0], recv_sem.at[0])
    local.start()
    copies = []
    for offset in OFFSETS:
        slot = slot_number(offset)
        copy = pltpu.make_async_remote_copy(
            send.at[slot], arrived.at[slot], send_sem.at[slot], recv_sem.at[slot],
            device_id=(core, peer(offset, -1)), device_id_type=MESH,
        )
        copy.start()
        copies.append(copy)
    local.wait()
    for copy in copies:
        copy.wait()
    position = lax.broadcasted_iota(jnp.int32, (CELL, C), 0)
    for cell in range(CELLS_DEV):
        rows = arrived[slots[cell]].astype(jnp.float32)
        count = counts[cell // HALF_CELLS, cell % HALF_CELLS]
        out[cell] = jnp.where(position < count, rows, 0.0).astype(jnp.bfloat16)


def any_spec():
    return pl.BlockSpec(memory_space=pl.ANY)


def vmem_spec():
    return pl.BlockSpec(memory_space=pltpu.VMEM)


def smem_spec():
    return pl.BlockSpec(memory_space=pltpu.SMEM)


def shards(features, hilbert_rank, valid_count, norm_gains, w_qkv, w_out, w_up, w_down):
    slab = jax.ShapeDtypeStruct((SLOTS, CELL, C), jnp.bfloat16)
    label_shape = jax.ShapeDtypeStruct((SLOTS, 1, 128), jnp.int32)
    dma = pltpu.SemaphoreType.DMA
    send, labels, slots = pl.pallas_call(
        first_kernel,
        out_shape=(slab, label_shape, jax.ShapeDtypeStruct((CELLS_DEV,), jnp.int32)),
        in_specs=[smem_spec(), smem_spec(), vmem_spec(), vmem_spec(), any_spec(), any_spec()],
        out_specs=(vmem_spec(), vmem_spec(), smem_spec()),
        scratch_shapes=[
            pltpu.VMEM((CELLS_DEV * CELL + TM, C), jnp.float32),
            pltpu.VMEM((C, FF), jnp.bfloat16),
            pltpu.VMEM((FF, C), jnp.bfloat16),
            pltpu.SMEM((CELLS_DEV,), jnp.int32),
            pltpu.SMEM((SLOTS,), jnp.int32),
            dma((2,)),
        ],
        compiler_params=pltpu.CompilerParams(vmem_limit_bytes=VMEM_LIMIT),
        name="first",
    )(hilbert_rank, valid_count, features.reshape(CELLS_DEV * CELL, C), norm_gains, w_up, w_down)

    own, other, own_labels, other_labels = pl.pallas_call(
        forward_kernel,
        out_shape=(slab, slab, label_shape, label_shape),
        in_specs=[any_spec(), vmem_spec()],
        out_specs=(any_spec(), any_spec(), any_spec(), any_spec()),
        scratch_shapes=[
            pltpu.VMEM((SLOTS, CELL, C), jnp.bfloat16),
            pltpu.VMEM((SLOTS, 1, 128), jnp.int32),
            dma((SLOTS,)), dma((SLOTS,)), dma((SLOTS,)), dma((SLOTS,)),
            dma((SLOTS,)), dma((SLOTS,)), dma((SLOTS,)), dma((3,)),
        ],
        compiler_params=pltpu.CompilerParams(
            collective_id=0, has_side_effects=True, vmem_limit_bytes=VMEM_LIMIT
        ),
        name="forward",
    )(send, labels)

    send = pl.pallas_call(
        layer_kernel,
        out_shape=slab,
        in_specs=[smem_spec(), smem_spec(), vmem_spec(), vmem_spec(), vmem_spec()]
        + [any_spec()] * 4,
        out_specs=vmem_spec(),
        scratch_shapes=[
            pltpu.VMEM((2, PATCH_ROWS + 2 * TK, C), jnp.float32),
            pltpu.VMEM((GROUPS, PATCH_ROWS, GROUP_LANES), jnp.bfloat16),
            pltpu.VMEM((GROUPS, PATCH_ROWS, GROUP_LANES), jnp.bfloat16),
            pltpu.VMEM((GROUPS, PATCH_ROWS, 2 * GROUP_LANES), jnp.bfloat16),
            pltpu.VMEM((GROUPS, HALF_ROWS, GROUP_LANES), jnp.bfloat16),
            pltpu.VMEM((C, 3 * C), jnp.bfloat16),
            pltpu.VMEM((C, C), jnp.bfloat16),
            pltpu.VMEM((C, FF), jnp.bfloat16),
            pltpu.VMEM((FF, C), jnp.bfloat16),
            pltpu.SMEM((SLOTS,), jnp.int32),
            dma((4,)),
        ],
        compiler_params=pltpu.CompilerParams(vmem_limit_bytes=VMEM_LIMIT),
        name="layer",
    )(
        own_labels.reshape(SLOTS, 128), other_labels.reshape(SLOTS, 128), own, other, norm_gains,
        w_qkv, w_out, w_up, w_down,
    )

    out = pl.pallas_call(
        return_kernel,
        out_shape=jax.ShapeDtypeStruct((CELLS_DEV, CELL, C), jnp.bfloat16),
        in_specs=[smem_spec(), smem_spec(), any_spec()],
        out_specs=vmem_spec(),
        scratch_shapes=[
            pltpu.VMEM((SLOTS, CELL, C), jnp.bfloat16),
            dma((SLOTS,)), dma((SLOTS,)),
        ],
        compiler_params=pltpu.CompilerParams(
            collective_id=1, has_side_effects=True, vmem_limit_bytes=VMEM_LIMIT
        ),
        name="homeward",
    )(slots, valid_count, send)
    return out.reshape(features.shape)


def solution(mesh):
    in_specs = (
        P("cells", "patch", None),
        P("cells", "patch"),
        P("cells", "patch"),
        P(),
        P(),
        P(),
        P(),
        P(),
    )
    out_specs = P("cells", "patch", None)
    return jax.shard_map(shards, mesh=mesh, in_specs=in_specs, out_specs=out_specs, check_vma=False)
```

profile of v0, /device:TPU:1, one launch (start us, length us, event | category | flops | bytes accessed | tf_op | source)
XLA Modules:
  0.0 158.5 jit_solution(14732533792272978807)
XLA Ops:
  0.0 10.9 %first.1 = (bf16[64,32,512]{2,1,0:T(8,128)(2,1)}, s32[64,1,128]{2,1,0:T(1,128)}, s32[32]{0:T(128)}) custom-call(s32[2,16]{1,0:T(2,128)} %rank_ref.1, s32[2,16]{1,0:T(2,128)} %counts.1, bf16[1024,512]{1,0:T(8,128)(2,1)} %bitcast.5, f32[3,512]{1,0:T(4,128)} %gains.3, bf16[2,512,2048]{2,1,0:T(8,128)(2,1)} %up_hbm.3, bf16[2,2048,512]{2,1,0:T(8,128)(2,1)} %down_hbm.3), custom_call_target="tpu_custom_call" | custom-call | tf_op jit(solution)/shard_map/first/pallas_call | solution.py:398
  10.9 43.3 %forward.1 = (bf16[64,32,512]{2,1,0:T(8,128)(2,1)}, bf16[64,32,512]{2,1,0:T(8,128)(2,1)}, s32[64,1,128]{2,1,0:T(1,128)}, s32[64,1,128]{2,1,0:T(1,128)}) custom-call(bf16[64,32,512]{2,1,0:T(8,128)(2,1)} %get-tuple-element.13.send, s32[64,1,128]{2,1,0:T(1,128)} %get-tuple-element.14.labels), custom_call_target="tpu_custom_call" | custom-call | tf_op jit(solution)/shard_map/forward/pallas_call | solution.py:415
  54.3 49.7 %layer.1.send = bf16[64,32,512]{2,1,0:T(8,128)(2,1)} custom-call(s32[64,128]{1,0:T(8,128)} %bitcast.6, s32[64,128]{1,0:T(8,128)} %bitcast.7, bf16[64,32,512]{2,1,0:T(8,128)(2,1)} %get-tuple-element.17.own, bf16[64,32,512]{2,1,0:T(8,128)(2,1)} %get-tuple-element.18.other, f32[3,512]{1,0:T(4,128)} %gains.3, bf16[512,1536]{1,0:T(8,128)(2,1)} %qkv_hbm.1, ...), custom_call_target="tpu_custom_call" | custom-call | tf_op jit(solution)/shard_map/layer/pallas_call | solution.py:432
  104.0 52.2 %homeward.1 = bf16[32,32,512]{2,1,0:T(8,128)(2,1)} custom-call(s32[32]{0:T(128)} %get-tuple-element.12.slots, s32[2,16]{1,0:T(2,128)} %counts.1, bf16[64,32,512]{2,1,0:T(8,128)(2,1)} %layer.1.send), custom_call_target="tpu_custom_call" | custom-call | tf_op jit(solution)/shard_map/homeward/pallas_call | solution.py:458
  156.2 2.3 %copy.10 = bf16[2,512,512]{2,1,0:T(8,128)(2,1)} copy(bf16[2,512,512]{2,1,0:T(8,128)(2,1)} %bitcast.4) | data formatting | bytes 2097152
where the time goes:
time: 159 us; the launch traced here: 158 us
  Pallas kernels  156 us (98%)
  local copies, waits for them, and re-layouts  2.26 us (1%)
    pallas_call x1, Pallas kernels, shards(): pl.pallas_call(return_kernel, out_shape=jax.ShapeDtypeStruct((CELLS_DEV,...  52.2 us
    pallas_call x1, Pallas kernels, shards(): pl.pallas_call(layer_kernel, out_shape=slab, in_specs=[smem_spec(), smem_...  49.7 us
    pallas_call x1, Pallas kernels, shards(): pl.pallas_call(forward_kernel, out_shape=(slab, slab, label_shape, label_...  43.3 us
    pallas_call x1, Pallas kernels, shards(): pl.pallas_call(first_kernel, out_shape=(slab, label_shape, jax.ShapeDtype...  10.9 us

commit v1 on v0

--- a/solution.py
+++ b/solution.py
@@ -25,8 +25,9 @@
 GROUP_HEADS = 8
 DEPTH = 16
 TM = 128
-TQ = 64
+TQ = 32
 TK = 128
+STACK = GROUP_HEADS * TQ
 VMEM_LIMIT = 60 * 1024 * 1024
 
 OFFSETS = [o for o in itertools.product(range(SIDE), repeat=3) if o != (0, 0, 0)]
@@ -274,47 +275,63 @@
         normed = norm_rows(packed[patch, rows, :], gains[1:2, :])
         projected = jnp.dot(normed, w_qkv[...], preferred_element_type=jnp.float32)
         projected = projected.astype(jnp.bfloat16)
-        seen = lax.broadcasted_iota(jnp.int32, (TM, GROUP_LANES), 0) + base < key_count
+        seen = lax.broadcasted_iota(jnp.int32, (GROUP_LANES, TM), 1) + base < key_count
+        ones = lax.broadcasted_iota(jnp.int32, (DEPTH, TM), 1) + base < key_count
         for group in range(GROUPS):
             low = group * GROUP_LANES
             queries[group, rows, :] = projected[:, low : low + GROUP_LANES] * 0.25
             keys[group, rows, :] = projected[:, C + low : C + low + GROUP_LANES]
             value = projected[:, 2 * C + low : 2 * C + low + GROUP_LANES].astype(jnp.float32)
-            values[group, rows, :GROUP_LANES] = jnp.where(seen, value, 0.0).astype(jnp.bfloat16)
-            values[group, rows, GROUP_LANES:] = jnp.where(seen, 1.0, 0.0).astype(jnp.bfloat16)
-        return carry
+            values[group, :GROUP_LANES, rows] = jnp.where(seen, value.T, 0.0).astype(jnp.bfloat16)
+            values[group, GROUP_LANES:, rows] = jnp.where(ones, 1.0, 0.0).astype(jnp.bfloat16)
+        return carry
+
+    fold = lax.broadcasted_iota(jnp.int32, (TQ, STACK), 1) % TQ
+    fold = fold == lax.broadcasted_iota(jnp.int32, (TQ, STACK), 0)
+    fold = fold.astype(jnp.float32).astype(jnp.bfloat16)
+    block = lax.broadcasted_iota(jnp.int32, (GROUP_LANES, STACK), 0) // DEPTH
+    block = block == lax.broadcasted_iota(jnp.int32, (GROUP_LANES, STACK), 1) // TQ
 
     def attend(key_span, step, carry):
-        group = step % GROUPS
-        rows = pl.ds(pl.multiple_of((step // GROUPS) * TQ, TQ), TQ)
-        query = queries[group, rows, :].astype(jnp.float32)
-        stacked = jnp.concatenate([query * mask for mask in head_masks], axis=0)
-        scores = lax.dot_general(
-            stacked.astype(jnp.bfloat16), keys[group, :key_span, :],
-            (((1,), (1,)), ((), ())), preferred_element_type=jnp.float32,
-        )
-        highest = jnp.max(scores, axis=1, keepdims=True)
-        weights = jnp.exp(scores - highest).astype(jnp.bfloat16)
-        mixture = jnp.dot(weights, values[group, :key_span, :], preferred_element_type=jnp.float32)
-        top = jnp.zeros((TQ, GROUP_LANES), jnp.float32)
-        total = jnp.zeros((TQ, GROUP_LANES), jnp.float32)
-        for head in range(GROUP_HEADS):
-            part = mixture[head * TQ : (head + 1) * TQ, :]
-            chosen = lane == head
-            top = jnp.where(chosen, part[:, :GROUP_LANES], top)
-            total = jnp.where(chosen, part[:, GROUP_LANES:], total)
-        mixed[group, rows, :] = (top / total).astype(jnp.bfloat16)
+        rows = pl.ds(pl.multiple_of(step * TQ, TQ), TQ)
+
+        def score(group):
+            query = queries[group, rows, :].astype(jnp.float32)
+            stacked = jnp.concatenate([query * mask for mask in head_masks], axis=0)
+            return lax.dot_general(
+                keys[group, :key_span, :], stacked.astype(jnp.bfloat16),
+                (((1,), (1,)), ((), ())), preferred_element_type=jnp.float32,
+            )
+
+        def weigh(scores):
+            highest = jnp.max(scores, axis=0, keepdims=True)
+            return jnp.exp(scores - highest).astype(jnp.bfloat16)
+
+        def mix(group, weights):
+            mixture = jnp.dot(
+                values[group, :, :key_span], weights, preferred_element_type=jnp.float32
+            )
+            top = mixture[:GROUP_LANES] / mixture[GROUP_LANES : GROUP_LANES + 1]
+            return jnp.where(block, top, 0.0).astype(jnp.bfloat16)
+
+        def store(group, top):
+            low = group * GROUP_LANES
+            mixed[rows, low : low + GROUP_LANES] = lax.dot_general(
+                fold, top, (((1,), (1,)), ((), ())), preferred_element_type=jnp.float32
+            ).astype(jnp.bfloat16)
+
+        scores = [score(group) for group in range(GROUPS)]
+        weights = [weigh(value) for value in scores]
+        tops = [mix(group, value) for group, value in enumerate(weights)]
+        for group, top in enumerate(tops):
+            store(group, top)
         return carry
 
     def finish(patch, step, carry):
         rows = pl.ds(pl.multiple_of(step * TM, TM), TM)
-        middle = packed[patch, rows, :]
-        for group in range(GROUPS):
-            low = group * GROUP_LANES
-            middle = middle + jnp.dot(
-                mixed[group, rows, :], w_out[low : low + GROUP_LANES, :],
-                preferred_element_type=jnp.float32,
-            )
+        middle = packed[patch, rows, :] + jnp.dot(
+            mixed[rows, :], w_out[...], preferred_element_type=jnp.float32
+        )
         middle = middle.astype(jnp.bfloat16).astype(jnp.float32)
         packed[patch, rows, :] = mlp_rows(middle, gains[2:3, :], w_up[...], w_down[...])
         return carry
@@ -330,7 +347,7 @@
         packed[patch, pl.ds(pl.multiple_of(base + 8, 8), TK), :] = jnp.broadcast_to(spare[:1], (TK, C))
         key_tiles = (key_count + TK - 1) // TK
         lax.fori_loop(0, key_tiles, functools.partial(project, patch, key_count), 0)
-        steps = (query_count + TQ - 1) // TQ * GROUPS
+        steps = (query_count + TQ - 1) // TQ
         for tiles in range(1, PATCH_ROWS // TK + 1):
 
             @pl.when(key_tiles == tiles)
@@ -439,8 +456,8 @@
             pltpu.VMEM((2, PATCH_ROWS + 2 * TK, C), jnp.float32),
             pltpu.VMEM((GROUPS, PATCH_ROWS, GROUP_LANES), jnp.bfloat16),
             pltpu.VMEM((GROUPS, PATCH_ROWS, GROUP_LANES), jnp.bfloat16),
-            pltpu.VMEM((GROUPS, PATCH_ROWS, 2 * GROUP_LANES), jnp.bfloat16),
-            pltpu.VMEM((GROUPS, HALF_ROWS, GROUP_LANES), jnp.bfloat16),
+            pltpu.VMEM((GROUPS, GROUP_LANES + DEPTH, PATCH_ROWS), jnp.bfloat16),
+            pltpu.VMEM((HALF_ROWS, C), jnp.bfloat16),
             pltpu.VMEM((C, 3 * C), jnp.bfloat16),
             pltpu.VMEM((C, C), jnp.bfloat16),
             pltpu.VMEM((C, FF), jnp.bfloat16),

time: 159 us -> 144 us (0.906)
  Pallas kernels: 156 us -> 140 us
    pallas_call x1, Pallas kernels: 52.2 us -> 34.1 us  [shards(): pl.pallas_call(return_kernel, out_shape=jax.ShapeDtypeStruct((CELLS_DEV,...]
    pallas_call x1, Pallas kernels: 49.7 us -> 52.2 us  [shards(): pl.pallas_call(layer_kernel, out_shape=slab, in_specs=[smem_spec(), smem_...]
    pallas_call x1, Pallas kernels: 43.3 us -> 41.7 us  [shards(): pl.pallas_call(forward_kernel, out_shape=(slab, slab, label_shape, label_...]
where the time goes in v1:
time: 144 us; the launch traced here: 142 us
  Pallas kernels  140 us (97%)
  local copies, waits for them, and re-layouts  2.26 us (2%)
    pallas_call x1, Pallas kernels, shards(): pl.pallas_call(layer_kernel, out_shape=slab, in_specs=[smem_spec(), smem_...  52.2 us
    pallas_call x1, Pallas kernels, shards(): pl.pallas_call(forward_kernel, out_shape=(slab, slab, label_shape, label_...  41.7 us
    pallas_call x1, Pallas kernels, shards(): pl.pallas_call(return_kernel, out_shape=jax.ShapeDtypeStruct((CELLS_DEV,...  34.1 us
    pallas_call x1, Pallas kernels, shards(): pl.pallas_call(first_kernel, out_shape=(slab, label_shape, jax.ShapeDtype...  11.9 us

profile of v1, /device:TPU:1, one launch (start us, length us, event | category | flops | bytes accessed | tf_op | source)
XLA Modules:
  0.0 142.2 jit_solution(5491025290837338593)
XLA Ops:
  0.0 11.9 %first.1 = (bf16[64,32,512]{2,1,0:T(8,128)(2,1)}, s32[64,1,128]{2,1,0:T(1,128)}, s32[32]{0:T(128)}) custom-call(s32[2,16]{1,0:T(2,128)} %rank_ref.1, s32[2,16]{1,0:T(2,128)} %counts.1, bf16[1024,512]{1,0:T(8,128)(2,1)} %bitcast.5, f32[3,512]{1,0:T(4,128)} %gains.3, bf16[2,512,2048]{2,1,0:T(8,128)(2,1)} %up_hbm.3, bf16[2,2048,512]{2,1,0:T(8,128)(2,1)} %down_hbm.3), custom_call_target="tpu_custom_call" | custom-call | tf_op jit(solution)/shard_map/first/pallas_call | solution.py:415
  11.9 41.7 %forward.1 = (bf16[64,32,512]{2,1,0:T(8,128)(2,1)}, bf16[64,32,512]{2,1,0:T(8,128)(2,1)}, s32[64,1,128]{2,1,0:T(1,128)}, s32[64,1,128]{2,1,0:T(1,128)}) custom-call(bf16[64,32,512]{2,1,0:T(8,128)(2,1)} %get-tuple-element.13.send, s32[64,1,128]{2,1,0:T(1,128)} %get-tuple-element.14.labels), custom_call_target="tpu_custom_call" | custom-call | tf_op jit(solution)/shard_map/forward/pallas_call | solution.py:432
  53.6 52.2 %layer.1.send = bf16[64,32,512]{2,1,0:T(8,128)(2,1)} custom-call(s32[64,128]{1,0:T(8,128)} %bitcast.6, s32[64,128]{1,0:T(8,128)} %bitcast.7, bf16[64,32,512]{2,1,0:T(8,128)(2,1)} %get-tuple-element.17.own, bf16[64,32,512]{2,1,0:T(8,128)(2,1)} %get-tuple-element.18.other, f32[3,512]{1,0:T(4,128)} %gains.3, bf16[512,1536]{1,0:T(8,128)(2,1)} %qkv_hbm.1, ...), custom_call_target="tpu_custom_call" | custom-call | tf_op jit(solution)/shard_map/layer/pallas_call | solution.py:449
  105.8 34.1 %homeward.1 = bf16[32,32,512]{2,1,0:T(8,128)(2,1)} custom-call(s32[32]{0:T(128)} %get-tuple-element.12.slots, s32[2,16]{1,0:T(2,128)} %counts.1, bf16[64,32,512]{2,1,0:T(8,128)(2,1)} %layer.1.send), custom_call_target="tpu_custom_call" | custom-call | tf_op jit(solution)/shard_map/homeward/pallas_call | solution.py:475
  139.9 2.3 %copy.10 = bf16[2,512,512]{2,1,0:T(8,128)(2,1)} copy(bf16[2,512,512]{2,1,0:T(8,128)(2,1)} %bitcast.4) | data formatting | bytes 2097152
